TPU v7x, 32 devices: a whole 2x2x4 slice. The times are simulated.
32 devices in a mesh: req: 4 (over z), mlp: 8 (over y, x, core).
Axes of the slice: x: 2, y: 2, z: 4, core: 2. Of those that a mesh axis runs over, the one named last changes fastest.
Arguments:
- tokens: bfloat16 [1024, 5120], P(('req', 'mlp')), may hold values from -6 to 6
- modulation: float32 [16, 6, 5120], P('req'), may hold values from -3 to 3
- lengths: int32 [4, 4], P('req'), may hold values from 1 to 160, 256 in all within a row
- request_adapter: int32 [16], P('req'), may hold values from 0 to 31
- adapter_storage: int32 [32], replicated, may hold values from 0 to 31, each once
- adapter_down_weight: bfloat16 [32, 5120, 32], P('mlp'), may hold values from -0.078125 to 0.078125
- adapter_up_maps: bfloat16 [32, 2, 16, 4096], P('mlp'), may hold values from -1.5 to 1.5
- input_projection: bfloat16 [4, 5120, 4096], P(None, None, 'mlp'), may hold values from -0.078125 to 0.078125
- query_key_gains: float32 [3, 4096], P(None, 'mlp'), may hold values from 0.1 to 1.9
- positions: int32 [3, 1024], P(None, 'req'), may hold values from 0 to 63
- block_page_lookup: int32 [4, 16], P('req'), may hold values from 0 to 15, each once within a row
- output_projection: bfloat16 [2, 4096, 5120], P(None, 'mlp'), may hold values from -0.09375 to 0.09375
- cross_norm_gain: float32 [5120], replicated, may hold values from 0.1 to 1.9
- text_token_cache: bfloat16 [2, 16, 512, 4096], P(None, 'req', None, 'mlp'), may hold values from -3 to 3
- feedforward_up: bfloat16 [5120, 8192], P('req', 'mlp'), may hold values from -0.078125 to 0.078125
- feedforward_down: bfloat16 [8192, 5120], P('mlp', 'req'), may hold values from -0.0625 to 0.0625
Outputs:
- layer_out: bfloat16 [1024, 5120], P(('req', 'mlp'))
- kv_pages: bfloat16 [2, 64, 16, 4096], P(None, 'req', None, 'mlp')
Inputs may be any that keep to these rules, and one draw needn't show every extreme that they name: `lengths`: row g lists the token counts of the 4 requests of group g in order; they fill the group's 256 positions, and the largest is 160. A permutation: adapter a is stored at index adapter_storage[a] of adapter_down_weight and adapter_up_maps. `block_page_lookup`: each row is a permutation of a group's 16 pages.
All inputs are finite; a program needn't handle non-finite values.
Results may differ from a plain program's by a relative error of at most 0.017.
Values may be sent and summed in bfloat16 or wider, within the bound.
A program may use at most 192 MiB of HBM per device.

v0:
```python
import math
import jax
import jax.numpy as jnp
from jax import lax
from jax.sharding import PartitionSpec as P

HD = 128
PAGE = 16
EPSILON = 1e-06


def as_sent(array):

    def short(part):
        return part.astype(jnp.bfloat16) if part.dtype == jnp.float32 else part

    return jax.tree.map(short, array)


def layer_norm(values):
    center = values - jnp.mean(values, axis=-1, keepdims=True)
    spread = jnp.mean(center * center, axis=-1, keepdims=True)
    return center * lax.rsqrt(spread + EPSILON)


def rotary_tables(grid):
    half_dim = HD // 2
    spatial = half_dim // 3
    temporal = half_dim - 2 * spatial
    column = jnp.arange(half_dim, dtype=jnp.int32)
    which_axis = jnp.where(
        column < temporal, 0, jnp.where(column < temporal + spatial, 1, 2)
    ).astype(jnp.int32)
    offset = jnp.where(
        which_axis == 0, 0, jnp.where(which_axis == 1, temporal, temporal + spatial)
    ).astype(jnp.int32)
    span_size = jnp.where(which_axis == 0, temporal, spatial).astype(jnp.float32)
    frequency = jnp.exp(-(column - offset).astype(jnp.float32) / span_size * math.log(10000.0))
    coordinate = grid.astype(jnp.float32)[which_axis, :].T
    angles = coordinate * frequency[None, :]
    return (jnp.cos(angles), jnp.sin(angles))


def rotate(values, cosine, sine_part):
    half_dim = HD // 2
    front_half = values[..., :half_dim]
    back_half = values[..., half_dim:]
    cosine = cosine[:, None, :]
    sine_part = sine_part[:, None, :]
    return jnp.concatenate(
        [front_half * cosine - back_half * sine_part, back_half * cosine + front_half * sine_part],
        axis=-1,
    )


def attend(queries, key_rows, value_rows, allowed):
    scores = jnp.einsum(
        "thd,shd->hts", queries, key_rows, preferred_element_type=jnp.float32
    ) / math.sqrt(HD)
    scores = jnp.where(allowed[None], scores, -1e30)
    weights = jnp.exp(scores)
    weights = (weights / jnp.sum(weights, axis=-1, keepdims=True)).astype(jnp.bfloat16)
    return jnp.einsum(
        "hts,shd->thd", weights, value_rows, preferred_element_type=jnp.float32
    ).astype(jnp.bfloat16)


def choose_rows(table, segment):
    chosen = jnp.zeros((segment.shape[0],) + table.shape[1:], table.dtype)
    for request in range(table.shape[0]):
        picked = (segment == request).reshape((-1,) + (1,) * (table.ndim - 1))
        chosen = jnp.where(picked, table[request][None], chosen)
    return chosen


def body(
    tokens,
    modulation,
    lengths,
    request_adapter,
    adapter_storage,
    adapter_down_weight,
    adapter_up_maps,
    input_projection,
    query_key_gains,
    positions,
    block_page_lookup,
    output_projection,
    cross_norm_gain,
    text_token_cache,
    feedforward_up,
    feedforward_down,
):
    mlp_count = lax.axis_size("mlp")
    my_index = lax.axis_index("mlp")
    own_count = tokens.shape[0]
    group_rows = own_count * mlp_count
    local_width = input_projection.shape[2]
    heads_local = local_width // HD
    entire_width = local_width * mlp_count
    resident_slots = adapter_down_weight.shape[0]
    doubled_rank = adapter_down_weight.shape[2]
    rank_once = doubled_rank // 2

    def over_group(own_rows, row_fn):
        return row_fn(lax.all_gather(own_rows, "mlp", axis=0, tiled=True), jnp.int32(0))

    def sum_rows(term_fn):
        return lax.psum_scatter(
            term_fn(jnp.int32(0), own_count * lax.axis_size("mlp")).astype(jnp.bfloat16),
            "mlp",
            scatter_dimension=0,
            tiled=True,
        ).astype(jnp.float32)

    def global_sum(pieces):
        return jax.tree.map(lambda part: part.astype(jnp.float32), lax.psum(as_sent(pieces), "mlp"))

    up_full, down_full = (
        lax.all_gather(feedforward_up, "req", axis=0, tiled=True),
        lax.all_gather(feedforward_down, "req", axis=1, tiled=True),
    )
    adapter_up_weight = lax.all_to_all(
        adapter_up_maps, "mlp", split_axis=3, concat_axis=0, tiled=True
    )
    slot_total = adapter_up_weight.shape[0]
    bounds = jnp.cumsum(lengths[0])
    position = jnp.arange(group_rows, dtype=jnp.int32)
    segment = jnp.sum((position[:, None] >= bounds[None, :]).astype(jnp.int32), axis=1)
    own_start = my_index * own_count
    own_segment = lax.dynamic_slice_in_dim(segment, own_start, own_count)
    per_token = [choose_rows(modulation[:, which_row, :], own_segment) for which_row in range(6)]
    token_f32 = tokens.astype(jnp.float32)
    normed_in = (layer_norm(token_f32) * (1.0 + per_token[1]) + per_token[0]).astype(jnp.bfloat16)

    def project_rows(incoming_rows, row_start):
        row_total = incoming_rows.shape[0]
        parts = [
            jnp.dot(incoming_rows, input_projection[which_map], preferred_element_type=jnp.float32)
            for which_map in range(3)
        ]
        code_block = jnp.einsum(
            "lf,sfe->lse", incoming_rows, adapter_down_weight, preferred_element_type=jnp.float32
        )
        parts.append(code_block.reshape(row_total, resident_slots * doubled_rank))
        return jnp.concatenate(parts, axis=1)

    projected = over_group(normed_in, project_rows)
    query_base = projected[:, :local_width]
    key_linear = projected[:, local_width : 2 * local_width]
    value_base = projected[:, 2 * local_width : 3 * local_width]
    code_block = projected[:, 3 * local_width :].reshape(group_rows, resident_slots, doubled_rank)
    request_slot = adapter_storage[request_adapter]
    token_slot = choose_rows(request_slot, segment)
    held = (
        token_slot[:, None]
        == my_index * resident_slots + jnp.arange(resident_slots, dtype=jnp.int32)[None, :]
    ).astype(jnp.float32)
    my_codes = jnp.sum(held[:, :, None] * code_block, axis=1)
    codes = global_sum(my_codes).astype(jnp.bfloat16)
    everywhere = (token_slot[:, None] == jnp.arange(slot_total, dtype=jnp.int32)[None, :]).astype(
        jnp.float32
    )

    def spread(code_part):
        return (
            (everywhere[:, :, None] * code_part[:, None, :].astype(jnp.float32))
            .reshape(group_rows, slot_total * rank_once)
            .astype(jnp.bfloat16)
        )

    query_up_weight = adapter_up_weight[:, 0].reshape(slot_total * rank_once, local_width)
    value_up_weight = adapter_up_weight[:, 1].reshape(slot_total * rank_once, local_width)
    query_linear = query_base + jnp.dot(
        spread(codes[:, :rank_once]), query_up_weight, preferred_element_type=jnp.float32
    )
    value_rows = (
        value_base
        + jnp.dot(spread(codes[:, rank_once:]), value_up_weight, preferred_element_type=jnp.float32)
    ).astype(jnp.bfloat16)
    query_square, key_square = global_sum(
        (jnp.sum(query_linear * query_linear, axis=1), jnp.sum(key_linear * key_linear, axis=1))
    )
    query_norm = (
        query_linear
        * lax.rsqrt(query_square / entire_width + EPSILON)[:, None]
        * query_key_gains[0]
    )
    key_norm = (
        key_linear * lax.rsqrt(key_square / entire_width + EPSILON)[:, None] * query_key_gains[1]
    )
    cosine, sine_part = rotary_tables(positions)
    query_rot = rotate(query_norm.reshape(group_rows, heads_local, HD), cosine, sine_part).astype(
        jnp.bfloat16
    )
    key_rot = rotate(key_norm.reshape(group_rows, heads_local, HD), cosine, sine_part).astype(
        jnp.bfloat16
    )
    value_heads = value_rows.reshape(group_rows, heads_local, HD)
    page_count = group_rows // PAGE
    stacked = jnp.stack(
        [
            key_rot.reshape(page_count, PAGE, local_width),
            value_rows.reshape(page_count, PAGE, local_width),
        ]
    )
    kv_pages = jnp.zeros_like(stacked).at[:, block_page_lookup[0]].set(stacked)
    allowed = segment[:, None] == segment[None, :]
    attended = attend(query_rot, key_rot, value_heads, allowed).reshape(group_rows, local_width)
    text_owner = (
        jnp.arange(text_token_cache.shape[1] * text_token_cache.shape[2], dtype=jnp.int32)
        // text_token_cache.shape[2]
    )
    cross_allowed = segment[:, None] == text_owner[None, :]
    text_keys = text_token_cache[0].reshape(-1, heads_local, HD)
    text_values = text_token_cache[1].reshape(-1, heads_local, HD)

    def attend_term(row_start, row_total):
        return jnp.dot(attended, output_projection[0], preferred_element_type=jnp.float32)

    first_res = (token_f32 + per_token[2] * sum_rows(attend_term)).astype(jnp.bfloat16)
    cross_own = (layer_norm(first_res.astype(jnp.float32)) * cross_norm_gain).astype(jnp.bfloat16)

    def cross_rows(incoming_rows, row_start):
        return jnp.dot(incoming_rows, input_projection[3], preferred_element_type=jnp.float32)

    cross_linear = over_group(cross_own, cross_rows)
    cross_square = global_sum(jnp.sum(cross_linear * cross_linear, axis=1))
    cross_query = (
        cross_linear
        * lax.rsqrt(cross_square / entire_width + EPSILON)[:, None]
        * query_key_gains[2]
    ).astype(jnp.bfloat16)
    cross_out = attend(
        cross_query.reshape(group_rows, heads_local, HD), text_keys, text_values, cross_allowed
    ).reshape(group_rows, local_width)

    def cross_term(row_start, row_total):
        return jnp.dot(cross_out, output_projection[1], preferred_element_type=jnp.float32)

    second_res = (first_res.astype(jnp.float32) + sum_rows(cross_term)).astype(jnp.bfloat16)
    mlp_own = (
        layer_norm(second_res.astype(jnp.float32)) * (1.0 + per_token[4]) + per_token[3]
    ).astype(jnp.bfloat16)

    def expand_rows(incoming_rows, row_start):
        return jax.nn.gelu(
            jnp.dot(incoming_rows, up_full, preferred_element_type=jnp.float32), approximate=True
        ).astype(jnp.bfloat16)

    hidden = over_group(mlp_own, expand_rows)

    def down_term(row_start, row_total):
        return jnp.dot(hidden, down_full, preferred_element_type=jnp.float32)

    layer_out = (second_res.astype(jnp.float32) + per_token[5] * sum_rows(down_term)).astype(
        jnp.bfloat16
    )
    return (layer_out, kv_pages)


def solution(mesh):
    return jax.shard_map(
        body,
        mesh=mesh,
        in_specs=(
            P(("req", "mlp"), None),
            P("req", None, None),
            P("req", None),
            P("req"),
            P(),
            P("mlp", None, None),
            P("mlp", None, None, None),
            P(None, None, "mlp"),
            P(None, "mlp"),
            P(None, "req"),
            P("req", None),
            P(None, "mlp", None),
            P(),
            P(None, "req", None, "mlp"),
            P("req", "mlp"),
            P("mlp", "req"),
        ),
        out_specs=(P(("req", "mlp"), None), P(None, "req", None, "mlp")),
        check_vma=False,
    )
```

profile of v0, /device:TPU:0, one launch (start us, length us, event | category | flops | bytes accessed | tf_op | source)
XLA Modules:
  0.0 720.8 jit_solution(13914493310342817437)
XLA Ops:
  8.1 2.6 fusion.93
  10.7 0.8 reduce-window.8
  11.7 1.1 convert_reduce_fusion.2
  12.9 1.2 fusion.48
  14.1 2.1 fusion.51
  16.2 11.0 %copy.88 = bf16[4,2,16,4096]{2,0,1,3:T(4,128)(2,1)} copy(bf16[4,2,16,4096]{3,2,1,0:T(8,128)(2,1)} %param.22) | data formatting | bytes 2097152 | tf_op args[6]
  27.2 11.3 %reshape.439 = bf16[8,2,32768]{2,1,0:T(2,128)(2,1)} reshape(bf16[4096,2,4,16]{3,2,1,0:T(4,128)(2,1)} %bitcast.123) | data formatting | bytes 2097152
  38.5 5.2 all-to-all-start
  43.8 0.6 gather_fusion
  44.4 0.7 gather_fusion.1
  45.1 0.7 fusion.96
  45.8 2.5 compare_select_fusion.10
  48.3 0.3 cosine_bitcast_fusion
  48.7 0.8 copy.94
  49.6 0.6 fusion.95
  50.2 0.6 fusion.67
  50.8 0.7 broadcast_compare_fusion.1
  51.5 8.3 %all-to-all-done = bf16[8,2,32768]{2,1,0:T(2,128)(2,1)S(1)} async-done(((bf16[8,2,32768]{2,1,0:T(2,128)(2,1)}), bf16[8,2,32768]{2,1,0:T(2,128)(2,1)S(1)}, u32[]{:S(2)}, u32[]{:S(2)}) %all-to-all-start) | async-done | bytes 1048608 | tf_op jit(solution)/shard_map/all_to_all | solution.py:123
  59.8 7.6 %reshape.440 = bf16[4096,2,4,16]{3,2,1,0:T(4,128)(2,1)} reshape(bf16[8,2,32768]{2,1,0:T(2,128)(2,1)S(1)} %all-to-all-done) | data formatting | bytes 2097152
  67.3 10.8 %copy.106 = bf16[4,2,16,8,512]{4,2,1,0,3:T(8,128)(2,1)S(1)} copy(bf16[4,2,16,8,512]{2,0,1,4,3:T(4,128)(2,1)} %bitcast.122) | data formatting | bytes 2097152 | tf_op jit(solution)/shard_map/all_to_all | solution.py:123
  78.2 2.7 fusion.99
  81.0 22.3 %psum.28 = bf16[256,32]{0,1:T(8,128)(2,1)S(1)} all-reduce(bf16[256,32]{0,1:T(8,128)(2,1)S(1)} %multiply_reduce_fusion.3), channel_id=1, replica_groups=mesh['req'=4,'mlp'=8] {'mlp'}, use_global_device_ids=true, to_apply=%region_5.6 | all-reduce | flops 8192 | bytes 32768 | tf_op jit(solution)/shard_map/psum | solution.py:117
  103.3 1.6 multiply_convert_fusion.1
  104.9 4.9 fusion.7
  109.8 0.4 multiply_reduce_fusion.2
  110.3 4.1 multiply_reduce_fusion.1
  114.4 12.0 %all-reduce = (bf16[256]{0:T(256)(128)(2,1)S(1)}, bf16[256]{0:T(256)(128)(2,1)S(1)}) all-reduce(bf16[256]{0:T(256)(128)(2,1)S(1)} %get-tuple-element.62, bf16[256]{0:T(256)(128)(2,1)S(1)} %get-tuple-element.64), channel_id=1, replica_groups=mesh['req'=4,'mlp'=8] {'mlp'}, use_global_device_ids=true, to_apply=%region_9.10 | all-reduce | flops 512 | bytes 2048 | tf_op jit(solution)/shard_map/psum | solution.py:117
  126.7 0.3 fusion.92
  127.4 0.3 fusion.91
  127.7 4.8 fusion.9
  132.6 0.3 fusion.23
  132.9 0.8 copy.107
  134.3 0.4 fusion.22
  134.7 1.3 convolution_convert_fusion.3
  136.1 5.6 convolution_convert_fusion.2
  141.7 1.2 fusion.94
  142.9 42.6 %reduce-scatter.4.cloned.1.call-done = bf16[32,5120]{1,0:T(8,128)(2,1)} async-done(((bf16[256,5120]{1,0:T(8,128)(2,1)}), bf16[32,5120]{1,0:T(8,128)(2,1)}) %reduce-scatter.4.cloned.1.call-update) | async-done | bytes 327696 | tf_op jit(solution)/shard_map/reduce_scatter | solution.py:109
  185.5 1.4 convert_reduce_fusion.1
  186.8 0.3 fusion.45
  187.1 0.9 fusion.47
  188.1 4.0 fusion.89
  192.1 4.0 reshape_squeeze.14
  196.1 2.1 reshape.438
  198.2 0.4 broadcast_compare_fusion
  198.6 19.7 %all-gather.8.cloned.1.call-done = bf16[256,5120]{1,0:T(8,128)(2,1)} async-done(((bf16[32,5120]{1,0:T(8,128)(2,1)}), bf16[256,5120]{1,0:T(8,128)(2,1)}) %all-gather.8.cloned.1.call-update) | async-done | bytes 2621456 | tf_op jit(solution)/shard_map/all_gather | solution.py:106
  218.3 5.6 multiply_reduce_fusion
  223.9 13.3 %psum.31 = bf16[256]{0:T(256)(128)(2,1)S(1)} all-reduce(bf16[256]{0:T(256)(128)(2,1)S(1)} %get-tuple-element.66), channel_id=1, replica_groups=mesh['req'=4,'mlp'=8] {'mlp'}, use_global_device_ids=true, to_apply=%region_15.16 | all-reduce | flops 256 | bytes 1024 | tf_op jit(solution)/shard_map/psum | solution.py:117
  237.3 6.4 fusion
  243.6 5.9 fusion.24
  249.6 3.1 convolution_convert_fusion.1
  252.8 0.5 all-gather.12.cloned.1.call-update
  253.4 0.5 all-gather.14.cloned.1.call-update
  254.0 42.6 %reduce-scatter.6.cloned.1.call-done = bf16[32,5120]{1,0:T(8,128)(2,1)} async-done(((bf16[256,5120]{1,0:T(8,128)(2,1)}), bf16[32,5120]{1,0:T(8,128)(2,1)}) %reduce-scatter.6.cloned.1.call-update) | async-done | bytes 327696 | tf_op jit(solution)/shard_map/reduce_scatter | solution.py:109
  296.6 1.2 convert_reduce_fusion
  297.8 0.3 fusion.41
  298.1 1.1 fusion.44
  299.3 0.3 reduce-scatter.8.cloned.1.call-start
  299.6 139.0 %all-gather.12.cloned.1.call-done = bf16[5120,1024]{1,0:T(8,128)(2,1)} async-done(((bf16[1280,1024]{1,0:T(8,128)(2,1)}), bf16[5120,1024]{1,0:T(8,128)(2,1)}) %all-gather.12.cloned.1.call-update) | async-done | bytes 10485776 | tf_op jit(solution)/shard_map/all_gather | solution.py:120
  438.6 183.4 %all-gather.14.cloned.1.call-done = bf16[1024,5120]{1,0:T(8,128)(2,1)} async-done(((bf16[1024,1280]{1,0:T(8,128)(2,1)}), bf16[1024,5120]{1,0:T(8,128)(2,1)}) %all-gather.14.cloned.1.call-update) | async-done | bytes 10485776 | tf_op jit(solution)/shard_map/all_gather | solution.py:121
  622.0 30.5 %all-gather.10.cloned.1.call-done = bf16[256,5120]{1,0:T(8,128)(2,1)} async-done(((bf16[32,5120]{1,0:T(8,128)(2,1)}), bf16[256,5120]{1,0:T(8,128)(2,1)}) %all-gather.10.cloned.1.call-update) | async-done | bytes 2621456 | tf_op jit(solution)/shard_map/all_gather | solution.py:106
  652.5 15.1 %convolution_convert_fusion = bf16[256,5120]{1,0:T(8,128)(2,1)} fusion(bf16[1024,5120]{1,0:T(8,128)(2,1)} %all-gather.14.cloned.1.call-done, bf16[256,5120]{1,0:T(8,128)(2,1)} %all-gather.10.cloned.1.call-done, bf16[5120,1024]{1,0:T(8,128)(2,1)} %all-gather.12.cloned.1.call-done), kind=kOutput, calls=%fused_computation.6 | convolution fusion | flops 5372379136 | bytes 26214400 | tf_op jit(solution)/shard_map/dot_general | solution.py:254
  668.2 1.2 scatter_fusion
  669.5 42.0 %reduce-scatter.8.cloned.1.call-done = bf16[32,5120]{1,0:T(8,128)(2,1)} async-done(((bf16[256,5120]{1,0:T(8,128)(2,1)}), bf16[32,5120]{1,0:T(8,128)(2,1)}) %reduce-scatter.8.cloned.1.call-update) | async-done | bytes 327696 | tf_op jit(solution)/shard_map/reduce_scatter | solution.py:109
  711.5 2.0 fusion.54
  (134 shorter events, 2.6 us)
Async XLA Ops:
  8.0 70.2 %copy-start = (bf16[4,5120,32]{1,2,0:T(8,128)(2,1)S(1)}, bf16[4,5120,32]{1,2,0:T(8,128)(2,1)}, u32[]{:S(2)}) copy-start(bf16[4,5120,32]{1,2,0:T(8,128)(2,1)} %param.21) | copy-start | bytes 3932164
  8.0 70.2 %all-gather.6.cloned.1.call-start = ((), (), s32[]{:S(2)}) async-start(), calls=%async_computation.4 | async-start | bytes 2949120 | tf_op jit(solution)/shard_map/all_gather | solution.py:106
  11.7 15.5 %copy-start.27 = (pred[32]{0:T(512)(128)(4,1)}, pred[32]{0:T(512)(128)(4,1)S(1)}, u32[]{:S(2)}) copy-start(pred[32]{0:T(512)(128)(4,1)S(1)} %get-tuple-element.60) | copy-start | bytes 100
  11.7 15.5 %copy-start.29 = (pred[32]{0:T(512)(128)(4,1)}, pred[32]{0:T(512)(128)(4,1)S(1)}, u32[]{:S(2)}) copy-start(pred[32]{0:T(512)(128)(4,1)S(1)} %get-tuple-element.61) | copy-start | bytes 100
  27.2 16.5 %copy-start.34 = (s32[3,256]{1,0:T(4,128)S(1)}, s32[3,256]{1,0:T(4,128)}, u32[]{:S(2)}) copy-start(s32[3,256]{1,0:T(4,128)} %param.25) | copy-start | bytes 9220
  27.2 16.6 %copy-start.36 = (s32[4]{0:T(128)S(1)}, s32[4]{0:T(128)}, u32[]{:S(2)}) copy-start(s32[4]{0:T(128)} %param.19) | copy-start | bytes 52
  27.2 16.6 %copy-start.2 = (s32[32]{0:T(128)S(1)}, s32[32]{0:T(128)}, u32[]{:S(2)}) copy-start(s32[32]{0:T(128)} %param.20) | copy-start | bytes 388
  27.2 22.4 %copy-start.33 = (f32[3,512]{1,0:T(4,128)S(1)}, f32[3,512]{1,0:T(4,128)}, u32[]{:S(2)}) copy-start(f32[3,512]{1,0:T(4,128)} %param.24) | copy-start | bytes 18436
  38.5 21.3 %all-to-all-start = ((bf16[8,2,32768]{2,1,0:T(2,128)(2,1)}), bf16[8,2,32768]{2,1,0:T(2,128)(2,1)S(1)}, u32[]{:S(2)}, u32[]{:S(2)}) async-start(bf16[8,2,32768]{2,1,0:T(2,128)(2,1)} %reshape.439), calls=%async_computation | async-start | bytes 2097152 | tf_op jit(solution)/shard_map/all_to_all | solution.py:123
  43.7 141.8 %reduce-scatter.4.cloned.1.call-start = ((), (), s32[]{:S(2)}) async-start(), calls=%async_computation.5 | async-start | bytes 2949120 | tf_op jit(solution)/shard_map/reduce_scatter | solution.py:109
  104.9 5.3 copy-start.4
  110.3 16.2 %copy-start.32 = (f32[1,512]{1,0:T(1,128)S(1)}, f32[1,512]{1,0:T(1,128)}, u32[]{:S(2)}) copy-start(f32[1,512]{1,0:T(1,128)} %get-tuple-element.54) | copy-start | bytes 6148
  110.3 16.8 %copy-start.31 = (f32[1,512]{1,0:T(1,128)S(1)}, f32[1,512]{1,0:T(1,128)}, u32[]{:S(2)}) copy-start(f32[1,512]{1,0:T(1,128)} %get-tuple-element.53) | copy-start | bytes 6148
  127.7 4.9 copy-start.13
  127.7 6.1 copy-start.12
  132.6 1.7 copy-start.14
  132.9 3.1 copy-start.5
  134.1 1.9 copy-start.7
  136.0 49.5 %copy-start.3 = (bf16[32,5120]{1,0:T(8,128)(2,1)S(1)}, bf16[32,5120]{1,0:T(8,128)(2,1)}, u32[]{:S(2)}) copy-start(bf16[32,5120]{1,0:T(8,128)(2,1)} %param.16) | copy-start | bytes 983044
  136.0 49.4 %copy-start.25 = (f32[1,1,5120]{2,0,1:T(1,128)S(1)}, f32[1,1,5120]{2,0,1:T(1,128)}, u32[]{:S(2)}) copy-start(f32[1,1,5120]{2,0,1:T(1,128)} %get-tuple-element.40) | copy-start | bytes 61444
  136.0 49.4 %copy-start.28 = (pred[32]{0:T(512)(128)(4,1)S(1)}, pred[32]{0:T(512)(128)(4,1)}, u32[]{:S(2)}) copy-start(pred[32]{0:T(512)(128)(4,1)} %copy-done.27) | copy-start | bytes 100
  136.0 49.4 %copy-start.30 = (pred[32]{0:T(512)(128)(4,1)S(1)}, pred[32]{0:T(512)(128)(4,1)}, u32[]{:S(2)}) copy-start(pred[32]{0:T(512)(128)(4,1)} %copy-done.29) | copy-start | bytes 100
  136.1 51.1 %copy-start.26 = (f32[5120]{0:T(1024)S(1)}, f32[5120]{0:T(1024)}, u32[]{:S(2)}) copy-start(f32[5120]{0:T(1024)} %param.28) | copy-start | bytes 61444
  141.7 76.6 %all-gather.8.cloned.1.call-start = ((), (), s32[]{:S(2)}) async-start(), calls=%async_computation.6 | async-start | bytes 2949120 | tf_op jit(solution)/shard_map/all_gather | solution.py:106
  188.1 108.6 %reduce-scatter.6.cloned.1.call-start = ((), (), s32[]{:S(2)}) async-start(), calls=%async_computation.7 | async-start | bytes 2949120 | tf_op jit(solution)/shard_map/reduce_scatter | solution.py:109
  198.6 38.6 %copy-start.10 = (bf16[2048,4,128]{2,1,0:T(4,128)(2,1)S(1)}, bf16[2048,4,128]{2,1,0:T(4,128)(2,1)}, u32[]{:S(2)}) copy-start(bf16[2048,4,128]{2,1,0:T(4,128)(2,1)} %reshape_squeeze.14) | copy-start | bytes 6291460
  198.6 38.6 %copy-start.35 = (f32[1,512]{1,0:T(1,128)S(1)}, f32[1,512]{1,0:T(1,128)}, u32[]{:S(2)}) copy-start(f32[1,512]{1,0:T(1,128)} %get-tuple-element.52) | copy-start | bytes 6148
  237.2 6.4 copy-start.9
  237.2 12.3 %slice-start = ((s8[10485760]{0:T(1024)(128)(4,1)}), s8[4194304]{0:T(1024)(128)(4,1)S(1)}, s32[]{:S(2)}) async-start(s8[10485760]{0:T(1024)(128)(4,1)} %bitcast.159), calls=%async_computation.12 | async-start | bytes 8388608
  243.6 5.9 slice-start.1
  243.6 5.9 slice-start.2
  252.7 45.3 %copy-start.15 = (f32[1,1,5120]{2,0,1:T(1,128)S(1)}, f32[1,1,5120]{2,0,1:T(1,128)}, u32[]{:S(2)}) copy-start(f32[1,1,5120]{2,0,1:T(1,128)} %get-tuple-element.23) | copy-start | bytes 61444
  252.7 45.3 %copy-start.16 = (f32[1,1,5120]{2,0,1:T(1,128)S(1)}, f32[1,1,5120]{2,0,1:T(1,128)}, u32[]{:S(2)}) copy-start(f32[1,1,5120]{2,0,1:T(1,128)} %get-tuple-element.24) | copy-start | bytes 61444
  252.7 45.4 %copy-start.17 = (f32[1,1,5120]{2,0,1:T(1,128)S(1)}, f32[1,1,5120]{2,0,1:T(1,128)}, u32[]{:S(2)}) copy-start(f32[1,1,5120]{2,0,1:T(1,128)} %get-tuple-element.25) | copy-start | bytes 61444
  252.7 45.4 %copy-start.18 = (f32[1,1,5120]{2,0,1:T(1,128)S(1)}, f32[1,1,5120]{2,0,1:T(1,128)}, u32[]{:S(2)}) copy-start(f32[1,1,5120]{2,0,1:T(1,128)} %get-tuple-element.26) | copy-start | bytes 61444
  252.8 45.4 %copy-start.19 = (f32[1,1,5120]{2,0,1:T(1,128)S(1)}, f32[1,1,5120]{2,0,1:T(1,128)}, u32[]{:S(2)}) copy-start(f32[1,1,5120]{2,0,1:T(1,128)} %get-tuple-element.27) | copy-start | bytes 61444
  252.8 45.4 %copy-start.20 = (f32[1,1,5120]{2,0,1:T(1,128)S(1)}, f32[1,1,5120]{2,0,1:T(1,128)}, u32[]{:S(2)}) copy-start(f32[1,1,5120]{2,0,1:T(1,128)} %get-tuple-element.28) | copy-start | bytes 61444
  252.8 185.8 %all-gather.12.cloned.1.call-start = ((), (), s32[]{:S(2)}) async-start(), calls=%async_computation.9 | async-start | bytes 13107200 | tf_op jit(solution)/shard_map/all_gather | solution.py:120
  253.4 368.7 %all-gather.14.cloned.1.call-start = ((), (), s32[]{:S(2)}) async-start(), calls=%async_computation.10 | async-start | bytes 13107200 | tf_op jit(solution)/shard_map/all_gather | solution.py:121
  254.0 398.6 %all-gather.10.cloned.1.call-start = ((), (), s32[]{:S(2)}) async-start(), calls=%async_computation.8 | async-start | bytes 2949120 | tf_op jit(solution)/shard_map/all_gather | solution.py:106
  299.3 368.4 %copy-start.37 = (s32[1,16]{1,0:T(1,128)S(1)}, s32[1,16]{1,0:T(1,128)}, u32[]{:S(2)}) copy-start(s32[1,16]{1,0:T(1,128)} %param.26) | copy-start | bytes 196
  299.3 368.4 %copy-start.8 = (bf16[256,4,128]{2,0,1:T(8,128)(2,1)S(1)}, bf16[256,4,128]{2,0,1:T(8,128)(2,1)}, u32[]{:S(2)}) copy-start(bf16[256,4,128]{2,0,1:T(8,128)(2,1)} %copy-done.7) | copy-start | bytes 786436
  299.3 368.8 %copy-start.6 = (bf16[256,512]{1,0:T(8,128)(2,1)S(1)}, bf16[256,512]{1,0:T(8,128)(2,1)}, u32[]{:S(2)}) copy-start(bf16[256,512]{1,0:T(8,128)(2,1)} %copy-done.5) | copy-start | bytes 786436
  299.3 412.2 %reduce-scatter.8.cloned.1.call-start = ((), (), s32[]{:S(2)}) async-start(), calls=%async_computation.11 | async-start | bytes 2949120 | tf_op jit(solution)/shard_map/reduce_scatter | solution.py:109
  652.5 61.0 %copy-start.1 = (bf16[4,5120,32]{1,2,0:T(8,128)(2,1)S(1)}, bf16[4,5120,32]{1,2,0:T(8,128)(2,1)}, u32[]{:S(2)}) copy-start(bf16[4,5120,32]{1,2,0:T(8,128)(2,1)} %param.21) | copy-start | bytes 3932164
  667.7 43.8 %copy-start.21 = (f32[1,1,5120]{2,0,1:T(1,128)S(1)}, f32[1,1,5120]{2,0,1:T(1,128)}, u32[]{:S(2)}) copy-start(f32[1,1,5120]{2,0,1:T(1,128)} %get-tuple-element.22) | copy-start | bytes 61444
  667.7 43.8 %copy-start.22 = (f32[1,1,5120]{2,0,1:T(1,128)S(1)}, f32[1,1,5120]{2,0,1:T(1,128)}, u32[]{:S(2)}) copy-start(f32[1,1,5120]{2,0,1:T(1,128)} %get-tuple-element.29) | copy-start | bytes 61444
  667.7 43.8 %copy-start.23 = (f32[1,1,5120]{2,0,1:T(1,128)S(1)}, f32[1,1,5120]{2,0,1:T(1,128)}, u32[]{:S(2)}) copy-start(f32[1,1,5120]{2,0,1:T(1,128)} %get-tuple-element.30) | copy-start | bytes 61444
  667.7 43.9 %copy-start.24 = (f32[1,1,5120]{2,0,1:T(1,128)S(1)}, f32[1,1,5120]{2,0,1:T(1,128)}, u32[]{:S(2)}) copy-start(f32[1,1,5120]{2,0,1:T(1,128)} %get-tuple-element.31) | copy-start | bytes 61444
  669.5 44.0 %copy-start.11 = (bf16[2,16,16,512]{3,2,1,0:T(8,128)(2,1)}, bf16[2,16,16,512]{3,2,1,0:T(8,128)(2,1)S(1)}, u32[]{:S(2)}) copy-start(bf16[2,16,16,512]{3,2,1,0:T(8,128)(2,1)S(1)} %scatter_fusion) | copy-start | bytes 1572868
Sparse Core Ops, SparseCore 0:
  16.3 33.5 all-gather.5
  141.8 43.6 reduce-scatter.3
  188.2 30.0 all-gather.7
  252.9 43.6 reduce-scatter.5
  667.8 43.6 reduce-scatter.7
Sparse Core Ops, SparseCore 1:
  254.8 183.7 all-gather.11
  440.1 181.9 all-gather.13
  624.4 28.1 all-gather.9
where the time goes:
time: 723 us; the launch traced here: 721 us
  waiting for transfers between devices  509 us (70%)
  local copies, waits for them, and re-layouts  61.7 us (9%)
  matrix products  60.8 us (8%)
  blocking collectives  47.6 us (7%)
  other arithmetic  19.5 us (3%)
  between operations  16.2 us (2%)
    all_gather x1, waiting for transfers between devices, body(): lax.all_gather(feedforward_down, 'req', axis=1, tiled=True)  183 us
    all_gather x1, waiting for transfers between devices, body(): lax.all_gather(feedforward_up, 'req', axis=0, tiled=True)  139 us
    reduce_scatter x3, waiting for transfers between devices, sum_rows(): lax.psum_scatter(term_fn(jnp.int32(0), own_count * lax.axis_size('mlp'))....  127 us
    all_gather x3, waiting for transfers between devices, over_group(): lax.all_gather(own_rows, 'mlp', axis=0, tiled=True)  50.2 us
    psum x3, blocking collectives, global_sum(): lax.psum(as_sent(pieces), 'mlp')  47.6 us
    unnamed x85, local copies, waits for them, and re-layouts  30 us
    dot_general x1, matrix products, down_term(): return jnp.dot(hidden, down_full, preferred_element_type=jnp.float32)  15.1 us
  transfers between devices with their start and end apart: 9, of which 8 were waited for; matrix products, arithmetic and copies ran while one was open for 9% of the time, Pallas kernels for 0%

commit v1 on v0

--- a/solution.py
+++ b/solution.py
@@ -120,8 +120,11 @@
         lax.all_gather(feedforward_up, "req", axis=0, tiled=True),
         lax.all_gather(feedforward_down, "req", axis=1, tiled=True),
     )
-    adapter_up_weight = lax.all_to_all(
-        adapter_up_maps, "mlp", split_axis=3, concat_axis=0, tiled=True
+    adapter_up_weight = jnp.concatenate(
+        lax.all_to_all(
+            jnp.stack(jnp.split(adapter_up_maps, lax.axis_size("mlp"), axis=3)), "mlp", 0, 0
+        ),
+        axis=0,
     )
     slot_total = adapter_up_weight.shape[0]
     bounds = jnp.cumsum(lengths[0])

time: 723 us -> 699 us (0.967)
  local copies, waits for them, and re-layouts: 61.7 us -> 32.8 us
    unnamed x85 -> x91, local copies, waits for them, and re-layouts: 30 us -> 11.2 us
    all_to_all x1 -> x0, local copies, waits for them, and re-layouts: 10.8 us -> none  [body(): lax.all_to_all(adapter_up_maps, 'mlp', split_axis=3, concat_axis=0, tiled...]
  transfers between devices with their start and end apart: 9 -> 9, of which waited for: 8 -> 8; matrix products, arithmetic and copies ran while one was open for 9% -> 5% of each run, Pallas kernels for 0% -> 0%
where the time goes in v1:
time: 699 us; the launch traced here: 698 us
  waiting for transfers between devices  516 us (74%)
  matrix products  59.8 us (9%)
  blocking collectives  48.8 us (7%)
  local copies, waits for them, and re-layouts  32.8 us (5%)
  other arithmetic  18.8 us (3%)
  between operations  16.2 us (2%)
    all_gather x1, waiting for transfers between devices, body(): lax.all_gather(feedforward_down, 'req', axis=1, tiled=True)  183 us
    all_gather x1, waiting for transfers between devices, body(): lax.all_gather(feedforward_up, 'req', axis=0, tiled=True)  139 us
    reduce_scatter x3, waiting for transfers between devices, sum_rows(): lax.psum_scatter(term_fn(jnp.int32(0), own_count * lax.axis_size('mlp'))....  128 us
    all_gather x3, waiting for transfers between devices, over_group(): lax.all_gather(own_rows, 'mlp', axis=0, tiled=True)  50.1 us
    psum x3, blocking collectives, global_sum(): lax.psum(as_sent(pieces), 'mlp')  48.8 us
    dot_general x1, matrix products, down_term(): return jnp.dot(hidden, down_full, preferred_element_type=jnp.float32)  15 us
    all_to_all x1, waiting for transfers between devices, body(): lax.all_to_all(jnp.stack(jnp.split(adapter_up_maps, lax.axis_size('mlp'),...  14.6 us
  transfers between devices with their start and end apart: 9, of which 8 were waited for; matrix products, arithmetic and copies ran while one was open for 5% of the time, Pallas kernels for 0%

profile of v1, /device:TPU:0, one launch (start us, length us, event | category | flops | bytes accessed | tf_op | source)
XLA Modules:
  0.0 698.4 jit_solution(1740659191225537501)
XLA Ops:
  8.1 2.7 fusion.93
  10.8 0.8 reduce-window.8
  11.8 1.1 convert_reduce_fusion.2
  12.9 1.2 fusion.48
  14.2 2.1 fusion.51
  16.3 1.6 bitcast_dynamic-update-slice_fusion.7
  17.8 1.6 bitcast_dynamic-update-slice_fusion.6
  19.4 1.6 bitcast_dynamic-update-slice_fusion.5
  21.0 1.6 bitcast_dynamic-update-slice_fusion.4
  22.5 1.6 bitcast_dynamic-update-slice_fusion.3
  24.1 1.6 bitcast_dynamic-update-slice_fusion.2
  25.7 1.6 bitcast_dynamic-update-slice_fusion.1
  27.2 1.6 bitcast_dynamic-update-slice_fusion
  28.8 5.2 all-to-all-start
  34.1 0.6 gather_fusion
  34.8 0.7 gather_fusion.1
  35.4 0.6 fusion.96
  36.1 2.5 compare_select_fusion.10
  38.6 0.3 cosine_bitcast_fusion
  39.0 0.8 copy.45
  39.9 0.6 fusion.95
  40.5 0.6 fusion.67
  41.1 0.7 broadcast_compare_fusion.1
  41.8 14.6 %all-to-all-done = bf16[8,4,2,16,512]{4,3,2,1,0:T(8,128)(2,1)S(1)} async-done(((bf16[8,4,2,16,512]{4,3,2,1,0:T(8,128)(2,1)}), bf16[8,4,2,16,512]{4,3,2,1,0:T(8,128)(2,1)S(1)}, u32[]{:S(2)}, u32[]{:S(2)}) %all-to-all-start) | async-done | bytes 1048608 | tf_op jit(solution)/shard_map/all_to_all | solution.py:124
  56.5 2.7 fusion.99
  59.3 23.9 %psum.28 = bf16[256,32]{0,1:T(8,128)(2,1)S(1)} all-reduce(bf16[256,32]{0,1:T(8,128)(2,1)S(1)} %multiply_reduce_fusion.3), channel_id=1, replica_groups=mesh['req'=4,'mlp'=8] {'mlp'}, use_global_device_ids=true, to_apply=%region_5.6 | all-reduce | flops 8192 | bytes 32768 | tf_op jit(solution)/shard_map/psum | solution.py:117
  83.2 0.8 multiply_convert_fusion.1
  84.0 4.9 fusion.7
  89.0 0.4 multiply_reduce_fusion.2
  89.4 4.1 multiply_reduce_fusion.1
  93.5 11.8 %all-reduce = (bf16[256]{0:T(256)(128)(2,1)S(1)}, bf16[256]{0:T(256)(128)(2,1)S(1)}) all-reduce(bf16[256]{0:T(256)(128)(2,1)S(1)} %get-tuple-element.62, bf16[256]{0:T(256)(128)(2,1)S(1)} %get-tuple-element.64), channel_id=1, replica_groups=mesh['req'=4,'mlp'=8] {'mlp'}, use_global_device_ids=true, to_apply=%region_9.10 | all-reduce | flops 512 | bytes 2048 | tf_op jit(solution)/shard_map/psum | solution.py:117
  105.7 0.3 fusion.92
  106.3 0.3 fusion.91
  106.7 4.8 fusion.9
  111.5 0.3 fusion.23
  112.5 0.4 fusion.22
  113.0 0.3 convolution_convert_fusion.3
  113.4 5.6 convolution_convert_fusion.2
  119.0 1.2 fusion.94
  120.2 43.1 %reduce-scatter.4.cloned.1.call-done = bf16[32,5120]{1,0:T(8,128)(2,1)} async-done(((bf16[256,5120]{1,0:T(8,128)(2,1)}), bf16[32,5120]{1,0:T(8,128)(2,1)}) %reduce-scatter.4.cloned.1.call-update) | async-done | bytes 327696 | tf_op jit(solution)/shard_map/reduce_scatter | solution.py:109
  163.2 1.4 convert_reduce_fusion.1
  164.9 0.9 fusion.47
  166.0 4.0 fusion.89
  170.0 4.0 reshape_squeeze.14
  174.0 2.1 reshape.442
  176.1 0.4 broadcast_compare_fusion
  176.5 19.5 %all-gather.8.cloned.1.call-done = bf16[256,5120]{1,0:T(8,128)(2,1)} async-done(((bf16[32,5120]{1,0:T(8,128)(2,1)}), bf16[256,5120]{1,0:T(8,128)(2,1)}) %all-gather.8.cloned.1.call-update) | async-done | bytes 2621456 | tf_op jit(solution)/shard_map/all_gather | solution.py:106
  196.1 5.6 multiply_reduce_fusion
  201.7 13.1 %psum.31 = bf16[256]{0:T(256)(128)(2,1)S(1)} all-reduce(bf16[256]{0:T(256)(128)(2,1)S(1)} %get-tuple-element.66), channel_id=1, replica_groups=mesh['req'=4,'mlp'=8] {'mlp'}, use_global_device_ids=true, to_apply=%region_15.16 | all-reduce | flops 256 | bytes 1024 | tf_op jit(solution)/shard_map/psum | solution.py:117
  214.8 6.5 fusion
  221.3 5.9 fusion.24
  227.3 3.1 convolution_convert_fusion.1
  230.5 0.5 all-gather.12.cloned.1.call-update
  231.1 0.5 all-gather.14.cloned.1.call-update
  231.7 42.6 %reduce-scatter.6.cloned.1.call-done = bf16[32,5120]{1,0:T(8,128)(2,1)} async-done(((bf16[256,5120]{1,0:T(8,128)(2,1)}), bf16[32,5120]{1,0:T(8,128)(2,1)}) %reduce-scatter.6.cloned.1.call-update) | async-done | bytes 327696 | tf_op jit(solution)/shard_map/reduce_scatter | solution.py:109
  274.3 1.2 convert_reduce_fusion
  275.8 1.1 fusion.44
  277.2 139.1 %all-gather.12.cloned.1.call-done = bf16[5120,1024]{1,0:T(8,128)(2,1)} async-done(((bf16[1280,1024]{1,0:T(8,128)(2,1)}), bf16[5120,1024]{1,0:T(8,128)(2,1)}) %all-gather.12.cloned.1.call-update) | async-done | bytes 10485776 | tf_op jit(solution)/shard_map/all_gather | solution.py:120
  416.3 183.4 %all-gather.14.cloned.1.call-done = bf16[1024,5120]{1,0:T(8,128)(2,1)} async-done(((bf16[1024,1280]{1,0:T(8,128)(2,1)}), bf16[1024,5120]{1,0:T(8,128)(2,1)}) %all-gather.14.cloned.1.call-update) | async-done | bytes 10485776 | tf_op jit(solution)/shard_map/all_gather | solution.py:121
  599.7 30.5 %all-gather.10.cloned.1.call-done = bf16[256,5120]{1,0:T(8,128)(2,1)} async-done(((bf16[32,5120]{1,0:T(8,128)(2,1)}), bf16[256,5120]{1,0:T(8,128)(2,1)}) %all-gather.10.cloned.1.call-update) | async-done | bytes 2621456 | tf_op jit(solution)/shard_map/all_gather | solution.py:106
  630.2 15.0 %convolution_convert_fusion = bf16[256,5120]{1,0:T(8,128)(2,1)} fusion(bf16[1024,5120]{1,0:T(8,128)(2,1)} %all-gather.14.cloned.1.call-done, bf16[256,5120]{1,0:T(8,128)(2,1)} %all-gather.10.cloned.1.call-done, bf16[5120,1024]{1,0:T(8,128)(2,1)} %all-gather.12.cloned.1.call-done), kind=kOutput, calls=%fused_computation.6 | convolution fusion | flops 5372379136 | bytes 26214400 | tf_op jit(solution)/shard_map/dot_general | solution.py:257
  645.8 1.2 scatter_fusion
  647.0 42.0 %reduce-scatter.8.cloned.1.call-done = bf16[32,5120]{1,0:T(8,128)(2,1)} async-done(((bf16[256,5120]{1,0:T(8,128)(2,1)}), bf16[32,5120]{1,0:T(8,128)(2,1)}) %reduce-scatter.8.cloned.1.call-update) | async-done | bytes 327696 | tf_op jit(solution)/shard_map/reduce_scatter | solution.py:109
  689.1 2.0 fusion.54
  (140 shorter events, 3.7 us)
Async XLA Ops:
  8.0 48.5 %copy-start = (bf16[4,5120,32]{1,2,0:T(8,128)(2,1)S(1)}, bf16[4,5120,32]{1,2,0:T(8,128)(2,1)}, u32[]{:S(2)}) copy-start(bf16[4,5120,32]{1,2,0:T(8,128)(2,1)} %param.21) | copy-start | bytes 3932164
  8.0 26.0 %copy-start.35 = (s32[3,256]{1,0:T(4,128)S(1)}, s32[3,256]{1,0:T(4,128)}, u32[]{:S(2)}) copy-start(s32[3,256]{1,0:T(4,128)} %param.25) | copy-start | bytes 9220
  8.0 26.1 %copy-start.37 = (s32[4]{0:T(128)S(1)}, s32[4]{0:T(128)}, u32[]{:S(2)}) copy-start(s32[4]{0:T(128)} %param.19) | copy-start | bytes 52
  8.0 26.1 %copy-start.2 = (s32[32]{0:T(128)S(1)}, s32[32]{0:T(128)}, u32[]{:S(2)}) copy-start(s32[32]{0:T(128)} %param.20) | copy-start | bytes 388
  8.0 48.5 %all-gather.6.cloned.1.call-start = ((), (), s32[]{:S(2)}) async-start(), calls=%async_computation.4 | async-start | bytes 2949120 | tf_op jit(solution)/shard_map/all_gather | solution.py:106
  8.1 31.8 %copy-start.34 = (f32[3,512]{1,0:T(4,128)S(1)}, f32[3,512]{1,0:T(4,128)}, u32[]{:S(2)}) copy-start(f32[3,512]{1,0:T(4,128)} %param.24) | copy-start | bytes 18436
  11.8 24.3 %copy-start.30 = (pred[32]{0:T(512)(128)(4,1)}, pred[32]{0:T(512)(128)(4,1)S(1)}, u32[]{:S(2)}) copy-start(pred[32]{0:T(512)(128)(4,1)S(1)} %get-tuple-element.61) | copy-start | bytes 100
  11.8 27.3 %copy-start.28 = (pred[32]{0:T(512)(128)(4,1)}, pred[32]{0:T(512)(128)(4,1)S(1)}, u32[]{:S(2)}) copy-start(pred[32]{0:T(512)(128)(4,1)S(1)} %get-tuple-element.60) | copy-start | bytes 100
  28.8 27.6 %all-to-all-start = ((bf16[8,4,2,16,512]{4,3,2,1,0:T(8,128)(2,1)}), bf16[8,4,2,16,512]{4,3,2,1,0:T(8,128)(2,1)S(1)}, u32[]{:S(2)}, u32[]{:S(2)}) async-start(bf16[8,4,2,16,512]{4,3,2,1,0:T(8,128)(2,1)} %bitcast_dynamic-update-slice_fusion), calls=%async_computation | async-start | bytes 2097152 | tf_op jit(solution)/shard_map/all_to_all | solution.py:124
  34.0 129.2 %reduce-scatter.4.cloned.1.call-start = ((), (), s32[]{:S(2)}) async-start(), calls=%async_computation.5 | async-start | bytes 2949120 | tf_op jit(solution)/shard_map/reduce_scatter | solution.py:109
  56.5 26.7 %copy-start.15 = (f32[256,32]{0,1:T(8,128)S(1)}, f32[256,32]{0,1:T(8,128)}, u32[]{:S(2)}) copy-start(f32[256,32]{0,1:T(8,128)} %fusion.67) | copy-start | bytes 98308
  84.0 5.3 copy-start.4
  89.4 16.0 %copy-start.33 = (f32[1,512]{1,0:T(1,128)S(1)}, f32[1,512]{1,0:T(1,128)}, u32[]{:S(2)}) copy-start(f32[1,512]{1,0:T(1,128)} %get-tuple-element.54) | copy-start | bytes 6148
  93.5 12.5 %copy-start.32 = (f32[1,512]{1,0:T(1,128)S(1)}, f32[1,512]{1,0:T(1,128)}, u32[]{:S(2)}) copy-start(f32[1,512]{1,0:T(1,128)} %get-tuple-element.53) | copy-start | bytes 6148
  106.7 4.9 copy-start.13
  106.7 5.4 copy-start.12
  111.5 1.0 copy-start.14
  111.9 1.4 copy-start.5
  112.3 1.0 copy-start.7
  113.3 49.9 %copy-start.3 = (bf16[32,5120]{1,0:T(8,128)(2,1)S(1)}, bf16[32,5120]{1,0:T(8,128)(2,1)}, u32[]{:S(2)}) copy-start(bf16[32,5120]{1,0:T(8,128)(2,1)} %param.16) | copy-start | bytes 983044
  113.3 49.9 %copy-start.26 = (f32[1,1,5120]{2,0,1:T(1,128)S(1)}, f32[1,1,5120]{2,0,1:T(1,128)}, u32[]{:S(2)}) copy-start(f32[1,1,5120]{2,0,1:T(1,128)} %get-tuple-element.40) | copy-start | bytes 61444
  113.3 49.9 %copy-start.29 = (pred[32]{0:T(512)(128)(4,1)S(1)}, pred[32]{0:T(512)(128)(4,1)}, u32[]{:S(2)}) copy-start(pred[32]{0:T(512)(128)(4,1)} %copy-done.28) | copy-start | bytes 100
  113.3 49.9 %copy-start.31 = (pred[32]{0:T(512)(128)(4,1)S(1)}, pred[32]{0:T(512)(128)(4,1)}, u32[]{:S(2)}) copy-start(pred[32]{0:T(512)(128)(4,1)} %copy-done.30) | copy-start | bytes 100
  118.9 46.0 %copy-start.27 = (f32[5120]{0:T(1024)S(1)}, f32[5120]{0:T(1024)}, u32[]{:S(2)}) copy-start(f32[5120]{0:T(1024)} %param.28) | copy-start | bytes 61444
  119.0 77.1 %all-gather.8.cloned.1.call-start = ((), (), s32[]{:S(2)}) async-start(), calls=%async_computation.6 | async-start | bytes 2949120 | tf_op jit(solution)/shard_map/all_gather | solution.py:106
  165.8 108.4 %reduce-scatter.6.cloned.1.call-start = ((), (), s32[]{:S(2)}) async-start(), calls=%async_computation.7 | async-start | bytes 2949120 | tf_op jit(solution)/shard_map/reduce_scatter | solution.py:109
  176.5 38.3 %copy-start.10 = (bf16[2048,4,128]{2,1,0:T(4,128)(2,1)S(1)}, bf16[2048,4,128]{2,1,0:T(4,128)(2,1)}, u32[]{:S(2)}) copy-start(bf16[2048,4,128]{2,1,0:T(4,128)(2,1)} %reshape_squeeze.14) | copy-start | bytes 6291460
  176.5 38.3 %copy-start.36 = (f32[1,512]{1,0:T(1,128)S(1)}, f32[1,512]{1,0:T(1,128)}, u32[]{:S(2)}) copy-start(f32[1,512]{1,0:T(1,128)} %get-tuple-element.52) | copy-start | bytes 6148
  214.8 6.5 copy-start.9
  214.8 12.4 %slice-start = ((s8[10485760]{0:T(1024)(128)(4,1)}), s8[4194304]{0:T(1024)(128)(4,1)S(1)}, s32[]{:S(2)}) async-start(s8[10485760]{0:T(1024)(128)(4,1)} %bitcast.167), calls=%async_computation.12 | async-start | bytes 8388608
  221.3 5.9 slice-start.1
  221.3 5.9 slice-start.2
  230.4 45.3 %copy-start.16 = (f32[1,1,5120]{2,0,1:T(1,128)S(1)}, f32[1,1,5120]{2,0,1:T(1,128)}, u32[]{:S(2)}) copy-start(f32[1,1,5120]{2,0,1:T(1,128)} %get-tuple-element.23) | copy-start | bytes 61444
  230.4 45.3 %copy-start.17 = (f32[1,1,5120]{2,0,1:T(1,128)S(1)}, f32[1,1,5120]{2,0,1:T(1,128)}, u32[]{:S(2)}) copy-start(f32[1,1,5120]{2,0,1:T(1,128)} %get-tuple-element.24) | copy-start | bytes 61444
  230.4 45.4 %copy-start.18 = (f32[1,1,5120]{2,0,1:T(1,128)S(1)}, f32[1,1,5120]{2,0,1:T(1,128)}, u32[]{:S(2)}) copy-start(f32[1,1,5120]{2,0,1:T(1,128)} %get-tuple-element.25) | copy-start | bytes 61444
  230.4 45.4 %copy-start.19 = (f32[1,1,5120]{2,0,1:T(1,128)S(1)}, f32[1,1,5120]{2,0,1:T(1,128)}, u32[]{:S(2)}) copy-start(f32[1,1,5120]{2,0,1:T(1,128)} %get-tuple-element.26) | copy-start | bytes 61444
  230.4 45.4 %copy-start.20 = (f32[1,1,5120]{2,0,1:T(1,128)S(1)}, f32[1,1,5120]{2,0,1:T(1,128)}, u32[]{:S(2)}) copy-start(f32[1,1,5120]{2,0,1:T(1,128)} %get-tuple-element.27) | copy-start | bytes 61444
  230.4 45.4 %copy-start.21 = (f32[1,1,5120]{2,0,1:T(1,128)S(1)}, f32[1,1,5120]{2,0,1:T(1,128)}, u32[]{:S(2)}) copy-start(f32[1,1,5120]{2,0,1:T(1,128)} %get-tuple-element.28) | copy-start | bytes 61444
  230.4 185.8 %all-gather.12.cloned.1.call-start = ((), (), s32[]{:S(2)}) async-start(), calls=%async_computation.9 | async-start | bytes 13107200 | tf_op jit(solution)/shard_map/all_gather | solution.py:120
  231.0 368.7 %all-gather.14.cloned.1.call-start = ((), (), s32[]{:S(2)}) async-start(), calls=%async_computation.10 | async-start | bytes 13107200 | tf_op jit(solution)/shard_map/all_gather | solution.py:121
  231.6 398.6 %all-gather.10.cloned.1.call-start = ((), (), s32[]{:S(2)}) async-start(), calls=%async_computation.8 | async-start | bytes 2949120 | tf_op jit(solution)/shard_map/all_gather | solution.py:106
  276.9 368.3 %copy-start.38 = (s32[1,16]{1,0:T(1,128)S(1)}, s32[1,16]{1,0:T(1,128)}, u32[]{:S(2)}) copy-start(s32[1,16]{1,0:T(1,128)} %param.26) | copy-start | bytes 196
  276.9 368.3 %copy-start.8 = (bf16[256,4,128]{2,0,1:T(8,128)(2,1)S(1)}, bf16[256,4,128]{2,0,1:T(8,128)(2,1)}, u32[]{:S(2)}) copy-start(bf16[256,4,128]{2,0,1:T(8,128)(2,1)} %copy-done.7) | copy-start | bytes 786436
  276.9 368.7 %copy-start.6 = (bf16[256,512]{1,0:T(8,128)(2,1)S(1)}, bf16[256,512]{1,0:T(8,128)(2,1)}, u32[]{:S(2)}) copy-start(bf16[256,512]{1,0:T(8,128)(2,1)} %copy-done.5) | copy-start | bytes 786436
  277.0 412.1 %reduce-scatter.8.cloned.1.call-start = ((), (), s32[]{:S(2)}) async-start(), calls=%async_computation.11 | async-start | bytes 2949120 | tf_op jit(solution)/shard_map/reduce_scatter | solution.py:109
  645.2 43.9 %copy-start.22 = (f32[1,1,5120]{2,0,1:T(1,128)S(1)}, f32[1,1,5120]{2,0,1:T(1,128)}, u32[]{:S(2)}) copy-start(f32[1,1,5120]{2,0,1:T(1,128)} %get-tuple-element.22) | copy-start | bytes 61444
  645.2 43.9 %copy-start.23 = (f32[1,1,5120]{2,0,1:T(1,128)S(1)}, f32[1,1,5120]{2,0,1:T(1,128)}, u32[]{:S(2)}) copy-start(f32[1,1,5120]{2,0,1:T(1,128)} %get-tuple-element.29) | copy-start | bytes 61444
  645.2 43.9 %copy-start.24 = (f32[1,1,5120]{2,0,1:T(1,128)S(1)}, f32[1,1,5120]{2,0,1:T(1,128)}, u32[]{:S(2)}) copy-start(f32[1,1,5120]{2,0,1:T(1,128)} %get-tuple-element.30) | copy-start | bytes 61444
  645.2 43.9 %copy-start.25 = (f32[1,1,5120]{2,0,1:T(1,128)S(1)}, f32[1,1,5120]{2,0,1:T(1,128)}, u32[]{:S(2)}) copy-start(f32[1,1,5120]{2,0,1:T(1,128)} %get-tuple-element.31) | copy-start | bytes 61444
  645.2 45.8 %copy-start.1 = (bf16[4,5120,32]{1,2,0:T(8,128)(2,1)S(1)}, bf16[4,5120,32]{1,2,0:T(8,128)(2,1)}, u32[]{:S(2)}) copy-start(bf16[4,5120,32]{1,2,0:T(8,128)(2,1)} %param.21) | copy-start | bytes 3932164
  647.0 44.0 %copy-start.11 = (bf16[2,16,16,512]{3,2,1,0:T(8,128)(2,1)}, bf16[2,16,16,512]{3,2,1,0:T(8,128)(2,1)S(1)}, u32[]{:S(2)}) copy-start(bf16[2,16,16,512]{3,2,1,0:T(8,128)(2,1)S(1)} %scatter_fusion) | copy-start | bytes 1572868
Sparse Core Ops, SparseCore 0:
  16.4 39.8 all-gather.5
  119.1 44.0 reduce-scatter.3
  165.9 30.0 all-gather.7
  230.6 43.6 reduce-scatter.5
  645.4 43.6 reduce-scatter.7
Sparse Core Ops, SparseCore 1:
  232.5 183.7 all-gather.11
  417.7 181.9 all-gather.13
  602.0 28.1 all-gather.9
